TPU v7x, 32 devices: a whole 2x2x4 slice. The times are simulated.
32 devices in a mesh: ep: 8 (over z, y), tp: 4 (over x, core).
Axes of the slice: x: 2, y: 2, z: 4, core: 2. Of those that a mesh axis runs over, the one named last changes fastest.
Arguments:
- hidden_in: bfloat16 [4096, 1536], P(('ep', 'tp')), may hold values from -6 to 6
- gain_attn: bfloat16 [1536], replicated, may hold values from 0.5 to 1.5
- w_query: bfloat16 [1536, 1536], P('tp'), may hold values from -0.15625 to 0.15625
- key_projection_weight: bfloat16 [512, 1536], P('tp'), may hold values from -0.15625 to 0.15625
- value_projection_weight: bfloat16 [512, 1536], P('tp'), may hold values from -0.15625 to 0.15625
- w_out: bfloat16 [1536, 1536], P('tp'), may hold values from -0.625 to 0.625
- gain_ffn: bfloat16 [1536], replicated, may hold values from 0.5 to 1.5
- w_router: bfloat16 [16, 1536], replicated, may hold values from -0.078125 to 0.078125
- w_gate: bfloat16 [16, 1536, 512], P('ep', None, 'tp'), may hold values from -0.15625 to 0.15625
- w_up: bfloat16 [16, 1536, 512], P('ep', None, 'tp'), may hold values from -0.15625 to 0.15625
- w_down: bfloat16 [16, 512, 1536], P('ep', 'tp'), may hold values from -0.75 to 0.75
- expert_ids: int32 [4096, 8], P('ep'), may hold values from 0 to 15, all different within a row; in each aligned block of 512 rows (0 to 511, 512 to 1023, ...) at most 512 rows name the same one
- slot_order: int32 [4096, 8], P('ep'), may hold values from 0 to 4095, as said below
- segment: int32 [4096], P('ep'), may hold values from 0 to 12, as said below
- position: int32 [4096], P('ep'), may hold values from 0 to 303, as said below
- cotangent: bfloat16 [4096, 1536], P(('ep', 'tp')), may hold values from -6 to 6
Outputs:
- output: bfloat16 [4096, 1536], P(('ep', 'tp'))
- grad_input: float32 [4096, 1536], P(('ep', 'tp'))
- grad_gain_attn: float32 [1536], replicated
- grad_query: float32 [1536, 1536], P('tp')
- grad_key: float32 [512, 1536], P('tp')
- grad_value: float32 [512, 1536], P('tp')
- grad_out: float32 [1536, 1536], P('tp')
- grad_gain_ffn: float32 [1536], replicated
- grad_router: float32 [16, 1536], replicated
- grad_gate: float32 [16, 1536, 512], P('ep', None, 'tp')
- grad_up: float32 [16, 1536, 512], P('ep', None, 'tp')
- grad_down: float32 [16, 512, 1536], P('ep', 'tp')
Inputs may be any that keep to these rules, and one draw needn't show every extreme that they name: `expert_ids`: in the 512 rows of one index of ep no expert is named by more than 512 rows, a bound that some block reaches of them. `slot_order`: within the 512 rows of one index of ep every number from 0 to 4095 appears once. Each tree is 512 consecutive tokens: its first 256 tokens are segment 0; segments 1 to 4 (branches, parent 0) hold 32 tokens each and segments 5 to 12 (leaves, parent 1 + (s - 5) // 2) hold 16 tokens each, each segment contiguous, in an order drawn for every tree. A token's position is its depth on its path: trunk 0 to 255, a branch from 256, a leaf from 288, rising by one along its segment.
All inputs are finite; a program needn't handle non-finite values.
Results may differ from a plain program's by a relative error of at most 0.02.
Values may be sent and summed in bfloat16 or wider, within the bound.
A program may use at most 320 MiB of HBM per device.

v0:
```python
import jax
import jax.numpy as jnp
from jax import lax
from jax.sharding import PartitionSpec as P

HEAD_DIMENSION = 64
TREE_TOKENS = 512
CAP = 2304
EPSILON = 1e-06
ROPE_BASE = 10000.0
EXACT_PRECISION = lax.Precision.HIGHEST


def rope_tables(position, head_width):
    half_width = head_width // 2
    freqs = ROPE_BASE ** (-(jnp.arange(half_width, dtype=jnp.float32) * 2.0 / head_width))
    angle = position.astype(jnp.float32)[:, None] * freqs[None, :]
    return (jnp.cos(angle)[:, None, :], jnp.sin(angle)[:, None, :])


def apply_rotation(value_rows, cosine_lookup, sine_lookup):
    half_width = value_rows.shape[-1] // 2
    first = value_rows[..., :half_width]
    second = value_rows[..., half_width:]
    return jnp.concatenate(
        [
            first * cosine_lookup - second * sine_lookup,
            first * sine_lookup + second * cosine_lookup,
        ],
        axis=-1,
    )


def rotate_back(grads, cosine_lookup, sine_lookup):
    half_width = grads.shape[-1] // 2
    first = grads[..., :half_width]
    second = grads[..., half_width:]
    return jnp.concatenate(
        [
            first * cosine_lookup + second * sine_lookup,
            second * cosine_lookup - first * sine_lookup,
        ],
        axis=-1,
    )


def norm_scale(value_rows):
    return lax.rsqrt(jnp.mean(value_rows * value_rows, axis=-1, keepdims=True) + EPSILON)


def norm_back(value_rows, scale, gain, grad_normed):
    weighted = grad_normed * gain
    inner = jnp.mean(value_rows * weighted, axis=-1, keepdims=True)
    grad_values = scale * weighted - value_rows * (scale * scale * scale) * inner
    return (grad_values, jnp.sum(grad_normed * value_rows * scale, axis=0))


def group_rows(value_rows):
    return lax.all_gather(value_rows, "tp", axis=0, tiled=True)


def group_totals(value_rows):
    return lax.psum_scatter(value_rows, "tp", scatter_dimension=0, tiled=True)


def gather_all(value_rows):
    return lax.all_gather(value_rows, ("ep", "tp"), axis=0, tiled=True)


def total_all(value_rows):
    return lax.psum_scatter(value_rows, ("ep", "tp"), scatter_dimension=0, tiled=True)


def kept_pairs(expert_ids, slot_order, expert_count, row_start, share):
    experts = jnp.arange(expert_count, dtype=jnp.int32)
    chosen = expert_ids[:, :, None] == experts[None, None, :]
    last = jnp.int32(1 << 30)
    order = jnp.min(jnp.where(chosen, slot_order[:, :, None], last), axis=1)
    counts = jnp.sum((order < last).astype(jnp.int32), axis=0)
    every = lax.all_gather(counts, "ep")
    earlier = jnp.arange(every.shape[0], dtype=jnp.int32) < lax.axis_index("ep")
    offsets = jnp.sum(jnp.where(earlier[:, None], every, 0), axis=0)
    own = lax.dynamic_slice_in_dim(order, row_start, share, 0)
    rank = jnp.sum((order[:, None, :] < own[None, :, :]).astype(jnp.int32), axis=0)
    used = own < last
    return (used, used & (rank + offsets[None, :] < CAP))


def visible_block(query_seg, query_pos, query_row, key_seg, key_pos, key_row):
    seg_q = query_seg[:, None]
    seg_k = key_seg[None, :]
    above = (
        (seg_k == seg_q)
        | (seg_k == 0)
        | (seg_k >= 1) & (seg_k <= 4) & (seg_q >= 5) & ((seg_q - 5) // 2 + 1 == seg_k)
    )
    same_tree = query_row[:, None] // TREE_TOKENS == key_row[None, :] // TREE_TOKENS
    return above & same_tree & (key_pos[None, :] <= query_pos[:, None])


def block_scores(query_part, key_rows, allowed, scale):
    scores = (
        jnp.einsum("qkgd,pkd->kgqp", query_part, key_rows, preferred_element_type=jnp.float32)
        * scale
    )
    return jnp.where(allowed[None, None], scores, -1e30)


def attend_forward(query_rows, key_rows, value_rows, segment, position):
    total_rows = query_rows.shape[0]
    scale = query_rows.shape[-1] ** (-0.5)
    row_ids = jnp.arange(total_rows, dtype=jnp.int32)
    allowed = visible_block(segment, position, row_ids, segment, position, row_ids)
    scores = block_scores(query_rows, key_rows, allowed, scale)
    top_score = jnp.max(scores, axis=-1, keepdims=True)
    weights = jnp.exp(scores - top_score)
    weight_sum = jnp.sum(weights, axis=-1, keepdims=True)
    probs = (weights / weight_sum).astype(jnp.bfloat16)
    outputs = jnp.einsum(
        "kgqp,pkd->qkgd", probs, value_rows, preferred_element_type=jnp.float32
    ).astype(jnp.bfloat16)
    log_sums = [top_score + jnp.log(weight_sum)]
    return (outputs, log_sums)


def attend_backward(
    query_rows, key_rows, value_rows, segment, position, log_sums, grad_heads, block_rows
):
    total_rows = query_rows.shape[0]
    scale = query_rows.shape[-1] ** (-0.5)
    row_ids = jnp.arange(total_rows, dtype=jnp.int32)
    grad_keys = jnp.zeros(key_rows.shape, jnp.float32)
    grad_values = jnp.zeros(value_rows.shape, jnp.float32)
    grad_query = []
    for number, first_row in enumerate(range(0, total_rows, block_rows)):
        allowed = visible_block(segment, position, row_ids, segment, position, row_ids)
        scores = block_scores(query_rows, key_rows, allowed, scale)
        probs = jnp.where(allowed[None, None], jnp.exp(scores - log_sums[number]), 0.0)
        grad_values = jnp.einsum(
            "kgqp,qkgd->pkd",
            probs.astype(jnp.bfloat16),
            grad_heads,
            preferred_element_type=jnp.float32,
        )
        grad_probs = jnp.einsum(
            "qkgd,pkd->kgqp", grad_heads, value_rows, preferred_element_type=jnp.float32
        )
        inner = jnp.sum(probs * grad_probs, axis=-1, keepdims=True)
        grad_scores = (probs * (grad_probs - inner)).astype(jnp.bfloat16)
        grad_query.append(
            jnp.einsum("kgqp,pkd->qkgd", grad_scores, key_rows, preferred_element_type=jnp.float32)
            * scale
        )
        grad_keys = (
            jnp.einsum(
                "kgqp,qkgd->pkd", grad_scores, query_rows, preferred_element_type=jnp.float32
            )
            * scale
        )
    return (grad_query[0], grad_keys, grad_values)


def local(
    hidden_in,
    gain_attn,
    w_query,
    key_projection_weight,
    value_projection_weight,
    w_out,
    gain_ffn,
    w_router,
    w_gate,
    w_up,
    w_down,
    expert_ids,
    slot_order,
    segment,
    position,
    cotangent,
):
    model_width = w_query.shape[1]
    head_width = HEAD_DIMENSION
    local_heads = w_query.shape[0] // head_width
    local_kv = key_projection_weight.shape[0] // head_width
    group_factor = local_heads // local_kv
    token_count = expert_ids.shape[0]
    share = hidden_in.shape[0]
    row_start = lax.axis_index("tp") * share
    expert_count = w_router.shape[0]
    per_owner = w_gate.shape[0]
    block_rows = 512
    used, kept = kept_pairs(expert_ids, slot_order, expert_count, row_start, share)
    cot_all = gather_all(cotangent)
    inputs_own = hidden_in.astype(jnp.float32)
    gain_one = gain_attn.astype(jnp.float32)
    gain_two = gain_ffn.astype(jnp.float32)
    scale_one = norm_scale(inputs_own)
    first_normalized = group_rows((inputs_own * scale_one * gain_one).astype(jnp.bfloat16))
    cosine_lookup, sine_lookup = rope_tables(position, head_width)
    query_proj = jnp.einsum(
        "rd,fd->rf", first_normalized, w_query, preferred_element_type=jnp.float32
    ).reshape(token_count, local_heads, head_width)
    key_proj = jnp.einsum(
        "rd,fd->rf", first_normalized, key_projection_weight, preferred_element_type=jnp.float32
    ).reshape(token_count, local_kv, head_width)
    query_rows = (
        apply_rotation(query_proj, cosine_lookup, sine_lookup)
        .astype(jnp.bfloat16)
        .reshape(token_count, local_kv, group_factor, head_width)
    )
    key_rows = apply_rotation(key_proj, cosine_lookup, sine_lookup).astype(jnp.bfloat16)
    value_rows = (
        jnp.einsum(
            "rd,fd->rf",
            first_normalized,
            value_projection_weight,
            preferred_element_type=jnp.float32,
        )
        .astype(jnp.bfloat16)
        .reshape(token_count, local_kv, head_width)
    )
    head_outputs, log_sums = attend_forward(query_rows, key_rows, value_rows, segment, position)
    head_outputs = head_outputs.reshape(token_count, local_heads * head_width)
    middle_own = inputs_own + group_totals(
        jnp.dot(head_outputs, w_out, preferred_element_type=jnp.float32)
    )
    scale_two = norm_scale(middle_own)
    normed_own = (middle_own * scale_two * gain_two).astype(jnp.bfloat16)
    normed_two = gather_all(normed_own)
    logits = jnp.einsum("rd,ed->re", normed_own, w_router, preferred_element_type=jnp.float32)
    top_logit = jnp.max(jnp.where(used, logits, -jnp.inf), axis=-1, keepdims=True)
    powers = jnp.where(used, jnp.exp(logits - top_logit), 0.0)
    gates = powers / jnp.sum(powers, axis=-1, keepdims=True)
    first_expert = lax.axis_index("ep") * per_owner
    kept_all = lax.dynamic_slice_in_dim(
        gather_all(kept.astype(jnp.float32)), first_expert, per_owner, 1
    )
    gate_all = lax.dynamic_slice_in_dim(
        gather_all(jnp.where(kept, gates, 0.0)), first_expert, per_owner, 1
    )
    units = w_gate.shape[2]
    gate_in = jnp.concatenate([w_gate[e] for e in range(per_owner)], axis=1)
    up_in = jnp.concatenate([w_up[e] for e in range(per_owner)], axis=1)
    down_in = w_down.reshape(per_owner * units, model_width)
    spread = jnp.repeat(gate_all, units, axis=1)
    gate_act = jnp.dot(normed_two, gate_in, preferred_element_type=jnp.float32)
    up_act = jnp.dot(normed_two, up_in, preferred_element_type=jnp.float32)
    back_act = jnp.einsum("rd,fd->rf", cot_all, down_in, preferred_element_type=jnp.float32)
    sigma = jax.nn.sigmoid(gate_act)
    hidden = gate_act * sigma * up_act
    weighted_hidden = (spread * hidden).astype(jnp.bfloat16)
    grad_hidden = spread * back_act
    grad_gate_act = (grad_hidden * up_act * sigma * (1.0 + gate_act * (1.0 - sigma))).astype(
        jnp.bfloat16
    )
    grad_up_act = (grad_hidden * gate_act * sigma).astype(jnp.bfloat16)
    grad_gates_part = kept_all * jnp.sum((hidden * back_act).reshape(-1, per_owner, units), axis=2)
    grad_rows = (
        jnp.einsum("rf,df->rd", grad_gate_act, gate_in, preferred_element_type=jnp.float32)
        + jnp.einsum("rf,df->rd", grad_up_act, up_in, preferred_element_type=jnp.float32)
    ).astype(jnp.bfloat16)
    grad_normed_own = total_all(grad_rows).astype(jnp.float32)
    grad_gates_own = total_all(
        lax.dynamic_update_slice_in_dim(
            jnp.zeros((normed_two.shape[0], expert_count), jnp.float32),
            grad_gates_part,
            first_expert,
            1,
        )
    )
    combined = jnp.dot(weighted_hidden, down_in, preferred_element_type=jnp.float32).astype(
        jnp.bfloat16
    )
    output_own = (middle_own + total_all(combined).astype(jnp.float32)).astype(jnp.bfloat16)
    grad_w_gate = jnp.einsum(
        "rd,ref->edf",
        normed_two,
        grad_gate_act.reshape(-1, per_owner, units),
        preferred_element_type=jnp.float32,
    )
    grad_w_up = jnp.einsum(
        "rd,ref->edf",
        normed_two,
        grad_up_act.reshape(-1, per_owner, units),
        preferred_element_type=jnp.float32,
    )
    grad_w_down = jnp.einsum(
        "rf,rd->fd", weighted_hidden, cot_all, preferred_element_type=jnp.float32
    ).reshape(per_owner, units, model_width)
    inner_gate = jnp.sum(gates * grad_gates_own, axis=-1, keepdims=True)
    grad_logits = gates * (grad_gates_own - inner_gate)
    router_f = w_router.astype(jnp.float32)
    grad_normed_own = grad_normed_own + jnp.dot(grad_logits, router_f, precision=EXACT_PRECISION)
    grad_router = jnp.dot(grad_logits.T, normed_own.astype(jnp.float32), precision=EXACT_PRECISION)
    grad_middle_back, grad_gain_ffn = norm_back(middle_own, scale_two, gain_two, grad_normed_own)
    grad_middle = cotangent.astype(jnp.float32) + grad_middle_back
    grad_attn = group_rows(grad_middle.astype(jnp.bfloat16))
    grad_w_out = jnp.einsum(
        "rf,rd->fd", head_outputs, grad_attn, preferred_element_type=jnp.float32
    )
    grad_heads = (
        jnp.einsum("rd,fd->rf", grad_attn, w_out, preferred_element_type=jnp.float32)
        .astype(jnp.bfloat16)
        .reshape(token_count, local_kv, group_factor, head_width)
    )
    grad_query, grad_keys, grad_values = attend_backward(
        query_rows, key_rows, value_rows, segment, position, log_sums, grad_heads, block_rows
    )
    grad_query_proj = (
        rotate_back(
            grad_query.reshape(token_count, local_heads, head_width), cosine_lookup, sine_lookup
        )
        .astype(jnp.bfloat16)
        .reshape(token_count, local_heads * head_width)
    )
    grad_key_proj = (
        rotate_back(grad_keys, cosine_lookup, sine_lookup)
        .astype(jnp.bfloat16)
        .reshape(token_count, local_kv * head_width)
    )
    grad_value_proj = grad_values.astype(jnp.bfloat16).reshape(token_count, local_kv * head_width)
    grad_w_query = jnp.einsum(
        "rf,rd->fd", grad_query_proj, first_normalized, preferred_element_type=jnp.float32
    )
    grad_w_key = jnp.einsum(
        "rf,rd->fd", grad_key_proj, first_normalized, preferred_element_type=jnp.float32
    )
    grad_w_value = jnp.einsum(
        "rf,rd->fd", grad_value_proj, first_normalized, preferred_element_type=jnp.float32
    )
    grad_normed_one = jnp.einsum(
        "rf,fd->rd", grad_query_proj, w_query, preferred_element_type=jnp.float32
    )
    grad_normed_one = grad_normed_one + jnp.einsum(
        "rf,fd->rd", grad_key_proj, key_projection_weight, preferred_element_type=jnp.float32
    )
    grad_normed_one = grad_normed_one + jnp.einsum(
        "rf,fd->rd", grad_value_proj, value_projection_weight, preferred_element_type=jnp.float32
    )
    grad_one_own = group_totals(grad_normed_one)
    grad_inputs_back, grad_gain_attn = norm_back(inputs_own, scale_one, gain_one, grad_one_own)
    grad_input = grad_middle + grad_inputs_back
    grad_w_query, grad_w_key, grad_w_value, grad_w_out = (
        lax.psum(grad_w_query.astype(jnp.bfloat16), "ep").astype(jnp.float32),
        lax.psum(grad_w_key.astype(jnp.bfloat16), "ep").astype(jnp.float32),
        lax.psum(grad_w_value.astype(jnp.bfloat16), "ep").astype(jnp.float32),
        lax.psum(grad_w_out.astype(jnp.bfloat16), "ep").astype(jnp.float32),
    )
    grad_gain_attn, grad_gain_ffn, grad_router = lax.psum(
        (grad_gain_attn, grad_gain_ffn, grad_router), ("ep", "tp")
    )
    return (
        output_own,
        grad_input,
        grad_gain_attn,
        grad_w_query,
        grad_w_key,
        grad_w_value,
        grad_w_out,
        grad_gain_ffn,
        grad_router,
        grad_w_gate,
        grad_w_up,
        grad_w_down,
    )


def solution(mesh):
    placed = (
        P(("ep", "tp"), None),
        P(),
        P("tp", None),
        P("tp", None),
        P("tp", None),
        P("tp", None),
        P(),
        P(),
        P("ep", None, "tp"),
        P("ep", None, "tp"),
        P("ep", "tp", None),
        P("ep", None),
        P("ep", None),
        P("ep"),
        P("ep"),
        P(("ep", "tp"), None),
    )
    return jax.shard_map(
        local,
        mesh=mesh,
        in_specs=placed,
        out_specs=(
            P(("ep", "tp"), None),
            P(("ep", "tp"), None),
            P(),
            P("tp", None),
            P("tp", None),
            P("tp", None),
            P("tp", None),
            P(),
            P(),
            P("ep", None, "tp"),
            P("ep", None, "tp"),
            P("ep", "tp", None),
        ),
        check_vma=False,
    )
```

profile of v0, /device:TPU:8, one launch (start us, length us, event | category | flops | bytes accessed | tf_op | source)
XLA Modules:
  0.0 1170.9 jit_solution(3175409998038890623)
XLA Ops:
  9.8 1.9 fusion.31
  15.8 16.9 %all-gather.6.cloned.1.call-done = bf16[512,1536]{1,0:T(8,128)(2,1)} async-done(((bf16[128,1536]{1,0:T(8,128)(2,1)}), bf16[512,1536]{1,0:T(8,128)(2,1)}) %all-gather.6.cloned.1.call-update) | async-done | bytes 1572880 | tf_op jit(solution)/shard_map/all_gather | solution.py:59
  32.7 2.1 fusion.66
  34.9 2.2 fusion.67
  44.2 2.6 fusion.68
  47.6 37.4 %reduce-scatter.6.cloned.1.call-done = f32[128,1536]{1,0:T(8,128)} async-done(((f32[512,1536]{1,0:T(8,128)}), f32[128,1536]{1,0:T(8,128)}) %reduce-scatter.6.cloned.1.call-update) | async-done | bytes 786448 | tf_op jit(solution)/shard_map/reduce_scatter | solution.py:63
  97.2 11.1 all-reduce
  111.0 4.3 convert_reduce_fusion
  116.7 36.5 %all_gather.30 = f32[4096,16]{0,1:T(8,128)} all-gather(f32[128,16]{0,1:T(8,128)S(1)} %get-tuple-element.48), channel_id=1, replica_groups=mesh['ep'=8,'tp'=4] {'ep','tp'}, dimensions={0}, use_global_device_ids=true | all-gather | bytes 270336 | tf_op jit(solution)/shard_map/all_gather | solution.py:67
  153.2 2.0 slice_bitcast_fusion.3
  155.2 2.0 slice_bitcast_fusion.1
  157.3 29.2 %all-gather.8.cloned.1.call-done = bf16[4096,1536]{1,0:T(8,128)(2,1)} async-done(((bf16[128,1536]{1,0:T(8,128)(2,1)}), bf16[4096,1536]{1,0:T(8,128)(2,1)}) %all-gather.8.cloned.1.call-update) | async-done | bytes 12582928 | tf_op jit(solution)/shard_map/all_gather | solution.py:67
  186.5 10.3 fusion.38
  196.8 10.2 fusion.40
  207.0 76.8 %all-gather.10.cloned.1.call-done = bf16[4096,1536]{1,0:T(8,128)(2,1)} async-done(((bf16[128,1536]{1,0:T(8,128)(2,1)}), bf16[4096,1536]{1,0:T(8,128)(2,1)}) %all-gather.10.cloned.1.call-update) | async-done | bytes 12582928 | tf_op jit(solution)/shard_map/all_gather | solution.py:67
  283.8 12.7 %bitcast_reduce_fusion = (f32[4096,2]{0,1:T(2,128)S(1)}, f32[4096,256]{0,1:T(8,128)}) fusion(f32[4096,256]{0,1:T(8,128)} %fusion.38, f32[4096,256]{0,1:T(8,128)} %fusion.40, bf16[4096,1536]{1,0:T(8,128)(2,1)} %all-gather.10.cloned.1.call-done, bf16[256,1536]{1,0:T(8,128)(2,1)} %bitcast.149), kind=kOutput, calls=%fused_computation.19 | convolution fusion | flops 3228557312 | bytes 25985024 | tf_op jit(solution)/shard_map/rd,fd->rf/dot_general | solution.py:248
  301.9 110.8 %reduce-scatter.12.cloned.1.call-done = f32[128,16]{0,1:T(8,128)} async-done(((f32[4096,16]{0,1:T(8,128)}), f32[128,16]{0,1:T(8,128)}) %reduce-scatter.12.cloned.1.call-update) | async-done | bytes 8208 | tf_op jit(solution)/shard_map/reduce_scatter | solution.py:71
  413.9 49.5 %all_gather.27 = f32[4096,16]{0,1:T(8,128)S(1)} all-gather(f32[128,16]{0,1:T(8,128)S(1)} %get-tuple-element.70), channel_id=1, replica_groups=mesh['ep'=8,'tp'=4] {'ep','tp'}, dimensions={0}, use_global_device_ids=true | all-gather | bytes 270336 | tf_op jit(solution)/shard_map/all_gather | solution.py:67
  463.5 7.3 multiply_convert_fusion
  470.8 10.4 fusion.39
  481.2 15.3 %add_convert_fusion = bf16[4096,1536]{1,0:T(8,128)(2,1)} fusion(f32[4096,1536]{1,0:T(8,128)} %fusion.39, bf16[4096,256]{0,1:T(8,128)(2,1)} %get-tuple-element.53, bf16[1536,128]{1,0:T(8,128)(2,1)} %get-tuple-element.64, bf16[1536,128]{1,0:T(8,128)(2,1)} %get-tuple-element.63), kind=kOutput, calls=%fused_computation | convolution fusion | flops 3235381248 | bytes 40632320 | tf_op jit(solution)/shard_map/rf,df->rd/dot_general | solution.py:260
  496.6 9.8 convolution_convert_fusion
  506.4 149.4 %reduce-scatter.10.cloned.1.call-done = bf16[128,1536]{1,0:T(8,128)(2,1)} async-done(((bf16[4096,1536]{1,0:T(8,128)(2,1)}), bf16[128,1536]{1,0:T(8,128)(2,1)}) %reduce-scatter.10.cloned.1.call-update) | async-done | bytes 393232 | tf_op jit(solution)/shard_map/reduce_scatter | solution.py:71
  655.7 3.2 multiply_reduce_fusion
  659.5 158.1 %reduce-scatter.8.cloned.1.call-done = bf16[128,1536]{1,0:T(8,128)(2,1)} async-done(((bf16[4096,1536]{1,0:T(8,128)(2,1)}), bf16[128,1536]{1,0:T(8,128)(2,1)}) %reduce-scatter.8.cloned.1.call-update) | async-done | bytes 393232 | tf_op jit(solution)/shard_map/reduce_scatter | solution.py:71
  817.6 2.9 fusion.62
  821.7 18.1 %all-gather.12.cloned.1.call-done = bf16[512,1536]{1,0:T(8,128)(2,1)} async-done(((bf16[128,1536]{1,0:T(8,128)(2,1)}), bf16[512,1536]{1,0:T(8,128)(2,1)}) %all-gather.12.cloned.1.call-update) | async-done | bytes 1572880 | tf_op jit(solution)/shard_map/all_gather | solution.py:59
  839.8 2.4 convolution_convert_fusion.5
  842.2 4.1 fusion.26
  846.4 4.5 fusion.4
  850.9 4.7 fusion.6
  858.2 1.8 convolution_convert_fusion.1
  862.2 1.8 convolution_convert_fusion.2
  864.2 2.3 fusion.69
  867.5 2.2 convolution_add_fusion
  870.0 7.2 fusion.17
  878.8 9.8 fusion.14
  888.7 3.1 copy.43
  892.7 9.8 fusion.70
  902.6 90.6 %all-reduce.8.cloned.1.call-done = (bf16[384,1536]{1,0:T(8,128)(2,1)}, bf16[128,1536]{1,0:T(8,128)(2,1)}, bf16[128,1536]{1,0:T(8,128)(2,1)}, bf16[384,1536]{1,0:T(8,128)(2,1)}) async-done(((bf16[384,1536]{1,0:T(8,128)(2,1)}, bf16[128,1536]{1,0:T(8,128)(2,1)}, bf16[128,1536]{1,0:T(8,128)(2,1)}, bf16[384,1536]{1,0:T(8,128)(2,1)}), (bf16[384,1536]{1,0:T(8,128)(2,1)}, bf16[128,1536]{1,0:T(8,128)(2,1)}, ...) | async-done | bytes 3145744 | tf_op jit(solution)/shard_map/psum | solution.py:344
  993.2 2.1 convert_element_type.156
  995.3 2.0 convert_element_type.158
  997.3 1.7 convert_element_type.154
  999.0 1.7 convert_element_type.160
  1000.7 33.4 %reduce-scatter.14.cloned.1.call-done = f32[128,1536]{1,0:T(8,128)} async-done(((f32[512,1536]{1,0:T(8,128)}), f32[128,1536]{1,0:T(8,128)}) %reduce-scatter.14.cloned.1.call-update) | async-done | bytes 786448 | tf_op jit(solution)/shard_map/reduce_scatter | solution.py:63
  1035.5 2.4 fusion.34
  1037.8 39.4 %all-reduce.1 = (f32[1536]{0:T(1024)}, f32[1536]{0:T(1024)}) all-reduce(f32[1536]{0:T(1024)S(1)} %get-tuple-element.38, f32[1536]{0:T(1024)S(1)} %copy-done.40), channel_id=1, replica_groups=mesh['ep'=8,'tp'=4] {'ep','tp'}, use_global_device_ids=true, to_apply=%region_21.22 | all-reduce | flops 3072 | bytes 24576 | tf_op jit(solution)/shard_map/psum | solution.py:349
  1077.3 85.3 %all-reduce.6.cloned.1.call-done = f32[16,1536]{1,0:T(8,128)} async-done(((f32[16,1536]{1,0:T(8,128)}), f32[16,1536]{1,0:T(8,128)}) %all-reduce.6.cloned.1.call-update) | async-done | bytes 98320 | tf_op jit(solution)/shard_map/psum | solution.py:349
  (181 shorter events, 50.0 us)
Async XLA Ops:
  7.2 37.1 %copy-start = (bf16[384,1536]{1,0:T(8,128)(2,1)S(1)}, bf16[384,1536]{1,0:T(8,128)(2,1)}, u32[]{:S(2)}) copy-start(bf16[384,1536]{1,0:T(8,128)(2,1)} %param.21) | copy-start | bytes 3538948
  7.2 27.7 %copy-start.20 = (bf16[384,1536]{1,0:T(8,128)(2,1)S(1)}, bf16[384,1536]{1,0:T(8,128)(2,1)}, u32[]{:S(2)}) copy-start(bf16[384,1536]{1,0:T(8,128)(2,1)} %param.18) | copy-start | bytes 3538948
  7.2 25.5 %all-gather.6.cloned.1.call-start = ((), (), s32[]{:S(2)}) async-start(), calls=%async_computation.5 | async-start | bytes 1966080 | tf_op jit(solution)/shard_map/all_gather | solution.py:59
  9.1 2.6 copy-start.46
  11.8 73.2 %reduce-scatter.6.cloned.1.call-start = ((), (), s32[]{:S(2)}) async-start(), calls=%async_computation.6 | async-start | bytes 3932160 | tf_op jit(solution)/shard_map/reduce_scatter | solution.py:63
  14.2 23.0 %copy-start.9 = (f32[512,32]{0,1:T(8,128)}, f32[512,32]{0,1:T(8,128)S(1)}, u32[]{:S(2)}) copy-start(f32[512,32]{0,1:T(8,128)S(1)} %get-tuple-element.71) | copy-start | bytes 196612
  14.2 23.0 %copy-start.11 = (f32[512,32]{0,1:T(8,128)}, f32[512,32]{0,1:T(8,128)S(1)}, u32[]{:S(2)}) copy-start(f32[512,32]{0,1:T(8,128)S(1)} %get-tuple-element.72) | copy-start | bytes 196612
  15.8 21.5 %copy-start.6 = (pred[512,512]{0,1:T(8,128)(4,1)}, pred[512,512]{0,1:T(8,128)(4,1)S(1)}, u32[]{:S(2)}) copy-start(pred[512,512]{0,1:T(8,128)(4,1)S(1)} %compare_and_fusion) | copy-start | bytes 786436
  34.9 2.5 copy-start.31
  34.9 2.5 copy-start.33
  38.6 3.6 copy-start.1
  38.6 3.6 copy-start.38
  38.6 2.6 copy-start.2
  38.6 3.0 copy-start.17
  46.9 139.6 %all-gather.8.cloned.1.call-start = ((), (), s32[]{:S(2)}) async-start(), calls=%async_computation.7 | async-start | bytes 12976128 | tf_op jit(solution)/shard_map/all_gather | solution.py:67
  47.6 107.7 %copy-start.35 = (f32[1536]{0:T(1024)}, f32[1536]{0:T(1024)S(1)}, u32[]{:S(2)}) copy-start(f32[1536]{0:T(1024)S(1)} %convert_element_type.133) | copy-start | bytes 18436
  88.5 195.3 %all-gather.10.cloned.1.call-start = ((), (), s32[]{:S(2)}) async-start(), calls=%async_computation.9 | async-start | bytes 12976128 | tf_op jit(solution)/shard_map/all_gather | solution.py:67
  89.1 323.6 %reduce-scatter.12.cloned.1.call-start = ((), (), s32[]{:S(2)}) async-start(), calls=%async_computation.11 | async-start | bytes 270336 | tf_op jit(solution)/shard_map/reduce_scatter | solution.py:71
  186.5 10.3 copy-start.13
  186.5 10.3 copy-start.15
  298.8 356.9 %reduce-scatter.10.cloned.1.call-start = ((), (), s32[]{:S(2)}) async-start(), calls=%async_computation.10 | async-start | bytes 12976128 | tf_op jit(solution)/shard_map/reduce_scatter | solution.py:71
  463.4 7.4 copy-start.14
  463.4 7.3 copy-start.16
  470.8 10.4 copy-start.3
  496.5 321.1 %reduce-scatter.8.cloned.1.call-start = ((), (), s32[]{:S(2)}) async-start(), calls=%async_computation.8 | async-start | bytes 12976128 | tf_op jit(solution)/shard_map/reduce_scatter | solution.py:71
  506.3 333.5 %all-gather.12.cloned.1.call-start = ((), (), s32[]{:S(2)}) async-start(), calls=%async_computation.12 | async-start | bytes 1966080 | tf_op jit(solution)/shard_map/all_gather | solution.py:59
  820.5 21.7 %copy-start.7 = (pred[512,512]{0,1:T(8,128)(4,1)S(1)}, pred[512,512]{0,1:T(8,128)(4,1)}, u32[]{:S(2)}) copy-start(pred[512,512]{0,1:T(8,128)(4,1)} %copy-done.6) | copy-start | bytes 786436
  820.5 172.7 %all-reduce.8.cloned.1.call-start = ((), (), s32[]{:S(2)}) async-start(), calls=%async_computation.15 | async-start | bytes 6291456 | tf_op jit(solution)/shard_map/psum | solution.py:344
  839.8 6.5 slice-start
  842.2 4.1 slice-start.1
  842.2 4.1 copy-start.30
  850.9 4.7 copy-start.26
  850.9 4.7 copy-start.28
  864.1 170.0 %reduce-scatter.14.cloned.1.call-start = ((), (), s32[]{:S(2)}) async-start(), calls=%async_computation.13 | async-start | bytes 3932160 | tf_op jit(solution)/shard_map/reduce_scatter | solution.py:63
  869.7 292.9 %all-reduce.6.cloned.1.call-start = ((), (), s32[]{:S(2)}) async-start(), calls=%async_computation.14 | async-start | bytes 196608 | tf_op jit(solution)/shard_map/psum | solution.py:349
  888.7 3.1 copy-start.5
  888.7 3.1 copy-start.36
  888.7 3.1 copy-start.37
  888.7 3.1 copy-start.42
  888.7 3.1 copy-start.43
  888.7 3.1 copy-start.45
  993.2 4.1 copy-start.22
  993.2 5.8 copy-start.21
  997.3 36.8 %copy-start.4 = (bf16[128,1536]{1,0:T(8,128)(2,1)S(1)}, bf16[128,1536]{1,0:T(8,128)(2,1)}, u32[]{:S(2)}) copy-start(bf16[128,1536]{1,0:T(8,128)(2,1)} %param.16) | copy-start | bytes 1179652
  997.3 36.8 %copy-start.47 = (f32[128]{0:T(128)S(1)}, f32[128]{0:T(128)}, u32[]{:S(2)}) copy-start(f32[128]{0:T(128)} %copy-done.46) | copy-start | bytes 1540
  999.0 36.5 %copy-start.8 = (f32[128,1536]{1,0:T(8,128)S(1)}, f32[128,1536]{1,0:T(8,128)}, u32[]{:S(2)}) copy-start(f32[128,1536]{1,0:T(8,128)} %get-tuple-element.47) | copy-start | bytes 2359300
  999.0 36.5 %copy-start.49 = (f32[128]{0:T(128)S(1)}, f32[128]{0:T(128)}, u32[]{:S(2)}) copy-start(f32[128]{0:T(128)} %get-tuple-element.76) | copy-start | bytes 1540
  999.0 38.9 %copy-start.40 = (f32[1536]{0:T(1024)S(1)}, f32[1536]{0:T(1024)}, u32[]{:S(2)}) copy-start(f32[1536]{0:T(1024)} %get-tuple-element.36) | copy-start | bytes 18436
  (16 other events, 20.0 us)
Sparse Core Ops, SparseCore 0:
  11.9 20.8 all-gather.5
  47.0 37.9 reduce-scatter.5
  88.9 97.5 all-gather.7
  189.6 94.2 all-gather.9
  299.0 113.6 reduce-scatter.11
  496.6 159.0 reduce-scatter.9
  662.8 154.7 reduce-scatter.7
  820.6 19.1 all-gather.11
  864.2 128.9 all-reduce.7
  995.8 38.2 reduce-scatter.13
  1040.3 122.3 all-reduce.5
where the time goes:
time: 1180 us; the launch traced here: 1170 us
  waiting for transfers between devices  807 us (68%)
  blocking collectives  136 us (12%)
  matrix products  135 us (11%)
  other arithmetic  53.1 us (4%)
  local copies, waits for them, and re-layouts  23.5 us (2%)
  between operations  15.4 us (1%)
    reduce_scatter x3, waiting for transfers between devices, total_all(): lax.psum_scatter(value_rows, ('ep', 'tp'), scatter_dimension=0, tiled=True)  418 us
    all_gather x2, waiting for transfers between devices, gather_all(): return lax.all_gather(value_rows, ('ep', 'tp'), axis=0, tiled=True)  106 us
    psum x1, waiting for transfers between devices, local(): lax.psum(grad_w_query.astype(jnp.bfloat16), 'ep').astype(jnp.float32)  90.6 us
    all_gather x2, blocking collectives, gather_all(): return lax.all_gather(value_rows, ('ep', 'tp'), axis=0, tiled=True)  86 us
    psum x1, waiting for transfers between devices, local(): lax.psum((grad_gain_attn, grad_gain_ffn, grad_router), ('ep', 'tp'))  85.3 us
    reduce_scatter x2, waiting for transfers between devices, group_totals(): return lax.psum_scatter(value_rows, 'tp', scatter_dimension=0, tiled=True)  70.9 us
    psum x1, blocking collectives, local(): lax.psum((grad_gain_attn, grad_gain_ffn, grad_router), ('ep', 'tp'))  39.4 us
    all_gather x2, waiting for transfers between devices, group_rows(): return lax.all_gather(value_rows, 'tp', axis=0, tiled=True)  35 us
  transfers between devices with their start and end apart: 11, of which 11 were waited for; matrix products, arithmetic and copies ran while one was open for 9% of the time, Pallas kernels for 0%

commit v1 on v0

--- a/solution.py
+++ b/solution.py
@@ -347,7 +347,7 @@
         lax.psum(grad_w_out.astype(jnp.bfloat16), "ep").astype(jnp.float32),
     )
     grad_gain_attn, grad_gain_ffn, grad_router = lax.psum(
-        (grad_gain_attn, grad_gain_ffn, grad_router), ("ep", "tp")
+        lax.psum((grad_gain_attn, grad_gain_ffn, grad_router), "tp"), "ep"
     )
     return (
         output_own,

time: 1180 us -> 1140 us (0.966)
  waiting for transfers between devices: 807 us -> 763 us
    psum x1 -> x2, waiting for transfers between devices: 85.3 us -> 24 us  [the longest x1 24 us: local(): lax.psum(lax.psum((grad_gain_attn, grad_gain_ffn, grad_router), 'tp'), 'ep')]
    psum x1, waiting for transfers between devices: 90.6 us -> 111 us  [local(): lax.psum(grad_w_query.astype(jnp.bfloat16), 'ep').astype(jnp.float32)]
    psum x1 -> x2, blocking collectives: 39.4 us -> 44.6 us  [the longest x1 34.1 us: local(): lax.psum(lax.psum((grad_gain_attn, grad_gain_ffn, grad_router), 'tp'), 'ep')]
  transfers between devices with their start and end apart: 11 -> 12, of which waited for: 11 -> 11; matrix products, arithmetic and copies ran while one was open for 9% -> 12% of each run, Pallas kernels for 0% -> 0%
where the time goes in v1:
time: 1140 us; the launch traced here: 1130 us
  waiting for transfers between devices  763 us (67%)
  blocking collectives  142 us (12%)
  matrix products  133 us (12%)
  other arithmetic  53 us (5%)
  local copies, waits for them, and re-layouts  22 us (2%)
  between operations  15.8 us (1%)
    reduce_scatter x3, waiting for transfers between devices, total_all(): lax.psum_scatter(value_rows, ('ep', 'tp'), scatter_dimension=0, tiled=True)  419 us
    psum x1, waiting for transfers between devices, local(): lax.psum(grad_w_query.astype(jnp.bfloat16), 'ep').astype(jnp.float32)  111 us
    all_gather x2, waiting for transfers between devices, gather_all(): return lax.all_gather(value_rows, ('ep', 'tp'), axis=0, tiled=True)  105 us
    all_gather x2, blocking collectives, gather_all(): return lax.all_gather(value_rows, ('ep', 'tp'), axis=0, tiled=True)  86.7 us
    reduce_scatter x2, waiting for transfers between devices, group_totals(): return lax.psum_scatter(value_rows, 'tp', scatter_dimension=0, tiled=True)  70.9 us
    psum x1, blocking collectives, local(): lax.psum(lax.psum((grad_gain_attn, grad_gain_ffn, grad_router), 'tp'), 'ep')  34.1 us
    all_gather x2, waiting for transfers between devices, group_rows(): return lax.all_gather(value_rows, 'tp', axis=0, tiled=True)  33.1 us
    psum x1, waiting for transfers between devices, local(): lax.psum(lax.psum((grad_gain_attn, grad_gain_ffn, grad_router), 'tp'), 'ep')  24 us
  transfers between devices with their start and end apart: 12, of which 11 were waited for; matrix products, arithmetic and copies ran while one was open for 12% of the time, Pallas kernels for 0%

profile of v1, /device:TPU:8, one launch (start us, length us, event | category | flops | bytes accessed | tf_op | source)
XLA Modules:
  0.0 1129.9 jit_solution(4868831586487369892)
XLA Ops:
  9.8 1.9 fusion.31
  15.8 16.9 %all-gather.6.cloned.1.call-done = bf16[512,1536]{1,0:T(8,128)(2,1)} async-done(((bf16[128,1536]{1,0:T(8,128)(2,1)}), bf16[512,1536]{1,0:T(8,128)(2,1)}) %all-gather.6.cloned.1.call-update) | async-done | bytes 1572880 | tf_op jit(solution)/shard_map/all_gather | solution.py:59
  32.7 2.1 fusion.66
  34.9 2.3 fusion.67
  44.2 2.6 fusion.68
  47.5 37.4 %reduce-scatter.6.cloned.1.call-done = f32[128,1536]{1,0:T(8,128)} async-done(((f32[512,1536]{1,0:T(8,128)}), f32[128,1536]{1,0:T(8,128)}) %reduce-scatter.6.cloned.1.call-update) | async-done | bytes 786448 | tf_op jit(solution)/shard_map/reduce_scatter | solution.py:63
  97.0 11.0 all-reduce
  110.9 4.3 convert_reduce_fusion
  116.5 37.3 %all_gather.30 = f32[4096,16]{0,1:T(8,128)} all-gather(f32[128,16]{0,1:T(8,128)S(1)} %get-tuple-element.50), channel_id=1, replica_groups=mesh['ep'=8,'tp'=4] {'ep','tp'}, dimensions={0}, use_global_device_ids=true | all-gather | bytes 270336 | tf_op jit(solution)/shard_map/all_gather | solution.py:67
  153.8 2.1 slice_bitcast_fusion.3
  155.9 2.0 slice_bitcast_fusion.1
  157.9 28.3 %all-gather.8.cloned.1.call-done = bf16[4096,1536]{1,0:T(8,128)(2,1)} async-done(((bf16[128,1536]{1,0:T(8,128)(2,1)}), bf16[4096,1536]{1,0:T(8,128)(2,1)}) %all-gather.8.cloned.1.call-update) | async-done | bytes 12582928 | tf_op jit(solution)/shard_map/all_gather | solution.py:67
  186.2 10.3 fusion.38
  196.5 10.2 fusion.40
  206.7 76.8 %all-gather.10.cloned.1.call-done = bf16[4096,1536]{1,0:T(8,128)(2,1)} async-done(((bf16[128,1536]{1,0:T(8,128)(2,1)}), bf16[4096,1536]{1,0:T(8,128)(2,1)}) %all-gather.10.cloned.1.call-update) | async-done | bytes 12582928 | tf_op jit(solution)/shard_map/all_gather | solution.py:67
  283.5 12.7 %bitcast_reduce_fusion = (f32[4096,2]{0,1:T(2,128)S(1)}, f32[4096,256]{0,1:T(8,128)}) fusion(f32[4096,256]{0,1:T(8,128)} %fusion.38, f32[4096,256]{0,1:T(8,128)} %fusion.40, bf16[4096,1536]{1,0:T(8,128)(2,1)} %all-gather.10.cloned.1.call-done, bf16[256,1536]{1,0:T(8,128)(2,1)} %bitcast.149), kind=kOutput, calls=%fused_computation.19 | convolution fusion | flops 3228557312 | bytes 25985024 | tf_op jit(solution)/shard_map/rd,fd->rf/dot_general | solution.py:248
  301.6 110.7 %reduce-scatter.12.cloned.1.call-done = f32[128,16]{0,1:T(8,128)} async-done(((f32[4096,16]{0,1:T(8,128)}), f32[128,16]{0,1:T(8,128)}) %reduce-scatter.12.cloned.1.call-update) | async-done | bytes 8208 | tf_op jit(solution)/shard_map/reduce_scatter | solution.py:71
  413.6 49.4 %all_gather.27 = f32[4096,16]{0,1:T(8,128)S(1)} all-gather(f32[128,16]{0,1:T(8,128)S(1)} %get-tuple-element.72), channel_id=1, replica_groups=mesh['ep'=8,'tp'=4] {'ep','tp'}, dimensions={0}, use_global_device_ids=true | all-gather | bytes 270336 | tf_op jit(solution)/shard_map/all_gather | solution.py:67
  463.0 7.3 multiply_convert_fusion
  470.4 10.4 fusion.39
  480.8 15.4 %add_convert_fusion = bf16[4096,1536]{1,0:T(8,128)(2,1)} fusion(f32[4096,1536]{1,0:T(8,128)} %fusion.39, bf16[4096,256]{0,1:T(8,128)(2,1)} %get-tuple-element.55, bf16[1536,128]{1,0:T(8,128)(2,1)} %get-tuple-element.66, bf16[1536,128]{1,0:T(8,128)(2,1)} %get-tuple-element.65), kind=kOutput, calls=%fused_computation | convolution fusion | flops 3235381248 | bytes 40632320 | tf_op jit(solution)/shard_map/rf,df->rd/dot_general | solution.py:260
  496.3 9.8 convolution_convert_fusion
  506.1 149.7 %reduce-scatter.10.cloned.1.call-done = bf16[128,1536]{1,0:T(8,128)(2,1)} async-done(((bf16[4096,1536]{1,0:T(8,128)(2,1)}), bf16[128,1536]{1,0:T(8,128)(2,1)}) %reduce-scatter.10.cloned.1.call-update) | async-done | bytes 393232 | tf_op jit(solution)/shard_map/reduce_scatter | solution.py:71
  655.8 3.3 multiply_reduce_fusion
  659.6 158.1 %reduce-scatter.8.cloned.1.call-done = bf16[128,1536]{1,0:T(8,128)(2,1)} async-done(((bf16[4096,1536]{1,0:T(8,128)(2,1)}), bf16[128,1536]{1,0:T(8,128)(2,1)}) %reduce-scatter.8.cloned.1.call-update) | async-done | bytes 393232 | tf_op jit(solution)/shard_map/reduce_scatter | solution.py:71
  817.7 2.9 fusion.62
  821.4 2.0 fusion.44
  823.7 16.2 %all-gather.12.cloned.1.call-done = bf16[512,1536]{1,0:T(8,128)(2,1)} async-done(((bf16[128,1536]{1,0:T(8,128)(2,1)}), bf16[512,1536]{1,0:T(8,128)(2,1)}) %all-gather.12.cloned.1.call-update) | async-done | bytes 1572880 | tf_op jit(solution)/shard_map/all_gather | solution.py:59
  839.9 2.4 convolution_convert_fusion.5
  842.3 4.1 fusion.26
  846.5 4.5 fusion.4
  851.0 4.7 fusion.6
  858.4 1.8 convolution_convert_fusion.1
  861.3 1.8 convolution_convert_fusion.2
  864.3 2.3 fusion.69
  867.7 2.2 convolution_add_fusion
  870.2 7.0 fusion.17
  878.9 7.0 fusion.14
  887.5 9.8 fusion.70
  897.4 110.6 %all-reduce.12.cloned.1.call-done = (bf16[384,1536]{1,0:T(8,128)(2,1)}, bf16[128,1536]{1,0:T(8,128)(2,1)}, bf16[128,1536]{1,0:T(8,128)(2,1)}, bf16[384,1536]{1,0:T(8,128)(2,1)}) async-done(((bf16[384,1536]{1,0:T(8,128)(2,1)}, bf16[128,1536]{1,0:T(8,128)(2,1)}, bf16[128,1536]{1,0:T(8,128)(2,1)}, bf16[384,1536]{1,0:T(8,128)(2,1)}), (bf16[384,1536]{1,0:T(8,128)(2,1)}, bf16[128,1536]{1,0:T(8,128)(2,1)}, ...) | async-done | bytes 3145744 | tf_op jit(solution)/shard_map/psum | solution.py:344
  1008.0 2.1 convert_element_type.156
  1010.1 2.0 convert_element_type.158
  1012.0 1.7 convert_element_type.154
  1015.4 33.4 %reduce-scatter.14.cloned.1.call-done = f32[128,1536]{1,0:T(8,128)} async-done(((f32[512,1536]{1,0:T(8,128)}), f32[128,1536]{1,0:T(8,128)}) %reduce-scatter.14.cloned.1.call-update) | async-done | bytes 786448 | tf_op jit(solution)/shard_map/reduce_scatter | solution.py:63
  1050.2 2.4 fusion.34
  1052.6 10.5 all-reduce.2
  1063.1 34.1 %all-reduce.1 = (f32[1536]{0:T(1024)}, f32[1536]{0:T(1024)}) all-reduce(f32[1536]{0:T(1024)S(1)} %get-tuple-element.42, f32[1536]{0:T(1024)S(1)} %get-tuple-element.43), channel_id=1, replica_groups=mesh['ep'=8,'tp'=4] {'ep'}, use_global_device_ids=true, to_apply=%region_22.23 | all-reduce | flops 3072 | bytes 24576 | tf_op jit(solution)/shard_map/psum | solution.py:349
  1097.2 24.0 %all-reduce.10.cloned.1.call-done = f32[16,1536]{1,0:T(8,128)} async-done(((f32[16,1536]{1,0:T(8,128)}), f32[16,1536]{1,0:T(8,128)}) %all-reduce.10.cloned.1.call-update) | async-done | bytes 98320 | tf_op jit(solution)/shard_map/psum | solution.py:349
  (173 shorter events, 52.2 us)
Async XLA Ops:
  7.2 37.0 %copy-start = (bf16[384,1536]{1,0:T(8,128)(2,1)S(1)}, bf16[384,1536]{1,0:T(8,128)(2,1)}, u32[]{:S(2)}) copy-start(bf16[384,1536]{1,0:T(8,128)(2,1)} %param.21) | copy-start | bytes 3538948
  7.2 27.6 %copy-start.19 = (bf16[384,1536]{1,0:T(8,128)(2,1)S(1)}, bf16[384,1536]{1,0:T(8,128)(2,1)}, u32[]{:S(2)}) copy-start(bf16[384,1536]{1,0:T(8,128)(2,1)} %param.18) | copy-start | bytes 3538948
  7.2 25.5 %all-gather.6.cloned.1.call-start = ((), (), s32[]{:S(2)}) async-start(), calls=%async_computation.5 | async-start | bytes 1966080 | tf_op jit(solution)/shard_map/all_gather | solution.py:59
  9.1 2.6 copy-start.40
  11.7 73.2 %reduce-scatter.6.cloned.1.call-start = ((), (), s32[]{:S(2)}) async-start(), calls=%async_computation.6 | async-start | bytes 3932160 | tf_op jit(solution)/shard_map/reduce_scatter | solution.py:63
  14.1 23.0 %copy-start.8 = (f32[512,32]{0,1:T(8,128)}, f32[512,32]{0,1:T(8,128)S(1)}, u32[]{:S(2)}) copy-start(f32[512,32]{0,1:T(8,128)S(1)} %get-tuple-element.73) | copy-start | bytes 196612
  14.2 23.0 %copy-start.10 = (f32[512,32]{0,1:T(8,128)}, f32[512,32]{0,1:T(8,128)S(1)}, u32[]{:S(2)}) copy-start(f32[512,32]{0,1:T(8,128)S(1)} %get-tuple-element.74) | copy-start | bytes 196612
  15.8 21.5 %copy-start.5 = (pred[512,512]{0,1:T(8,128)(4,1)}, pred[512,512]{0,1:T(8,128)(4,1)S(1)}, u32[]{:S(2)}) copy-start(pred[512,512]{0,1:T(8,128)(4,1)S(1)} %compare_and_fusion) | copy-start | bytes 786436
  34.8 2.5 copy-start.30
  34.8 2.5 copy-start.32
  38.5 3.6 copy-start.1
  38.6 3.6 copy-start.35
  38.6 2.6 copy-start.2
  38.6 3.0 copy-start.16
  41.5 1.9 copy-start.36
  46.8 139.4 %all-gather.8.cloned.1.call-start = ((), (), s32[]{:S(2)}) async-start(), calls=%async_computation.7 | async-start | bytes 12976128 | tf_op jit(solution)/shard_map/all_gather | solution.py:67
  47.5 108.4 %copy-start.34 = (f32[1536]{0:T(1024)}, f32[1536]{0:T(1024)S(1)}, u32[]{:S(2)}) copy-start(f32[1536]{0:T(1024)S(1)} %convert_element_type.133) | copy-start | bytes 18436
  88.4 195.1 %all-gather.10.cloned.1.call-start = ((), (), s32[]{:S(2)}) async-start(), calls=%async_computation.9 | async-start | bytes 12976128 | tf_op jit(solution)/shard_map/all_gather | solution.py:67
  88.9 323.4 %reduce-scatter.12.cloned.1.call-start = ((), (), s32[]{:S(2)}) async-start(), calls=%async_computation.11 | async-start | bytes 270336 | tf_op jit(solution)/shard_map/reduce_scatter | solution.py:71
  186.2 10.3 copy-start.12
  186.2 10.3 copy-start.14
  298.5 357.3 %reduce-scatter.10.cloned.1.call-start = ((), (), s32[]{:S(2)}) async-start(), calls=%async_computation.10 | async-start | bytes 12976128 | tf_op jit(solution)/shard_map/reduce_scatter | solution.py:71
  463.0 7.4 copy-start.13
  463.0 7.3 copy-start.15
  470.4 10.4 copy-start.3
  496.3 321.5 %reduce-scatter.8.cloned.1.call-start = ((), (), s32[]{:S(2)}) async-start(), calls=%async_computation.8 | async-start | bytes 12976128 | tf_op jit(solution)/shard_map/reduce_scatter | solution.py:71
  506.1 333.8 %all-gather.12.cloned.1.call-start = ((), (), s32[]{:S(2)}) async-start(), calls=%async_computation.12 | async-start | bytes 1966080 | tf_op jit(solution)/shard_map/all_gather | solution.py:59
  820.6 76.7 %all-reduce.8.cloned.1.call-start = ((), (), s32[]{:S(2)}) async-start(), calls=%async_computation.14 | async-start | bytes 196608 | tf_op jit(solution)/shard_map/psum | solution.py:350
  823.4 18.9 %copy-start.6 = (pred[512,512]{0,1:T(8,128)(4,1)S(1)}, pred[512,512]{0,1:T(8,128)(4,1)}, u32[]{:S(2)}) copy-start(pred[512,512]{0,1:T(8,128)(4,1)} %copy-done.5) | copy-start | bytes 786436
  823.4 184.5 %all-reduce.12.cloned.1.call-start = ((), (), s32[]{:S(2)}) async-start(), calls=%async_computation.16 | async-start | bytes 6291456 | tf_op jit(solution)/shard_map/psum | solution.py:344
  839.9 6.5 slice-start
  842.3 4.1 slice-start.1
  842.3 4.1 copy-start.29
  851.0 4.7 copy-start.25
  851.0 4.7 copy-start.27
  855.7 1.8 copy-start.9
  855.7 1.8 copy-start.11
  856.8 1.5 copy-start.44
  864.3 2.4 copy-start.18
  864.3 184.6 %reduce-scatter.14.cloned.1.call-start = ((), (), s32[]{:S(2)}) async-start(), calls=%async_computation.13 | async-start | bytes 3932160 | tf_op jit(solution)/shard_map/reduce_scatter | solution.py:63
  869.9 251.3 %all-reduce.10.cloned.1.call-start = ((), (), s32[]{:S(2)}) async-start(), calls=%async_computation.15 | async-start | bytes 196608 | tf_op jit(solution)/shard_map/psum | solution.py:349
  1008.0 4.1 copy-start.21
  1008.0 5.8 copy-start.20
  1012.0 36.8 %copy-start.4 = (bf16[128,1536]{1,0:T(8,128)(2,1)S(1)}, bf16[128,1536]{1,0:T(8,128)(2,1)}, u32[]{:S(2)}) copy-start(bf16[128,1536]{1,0:T(8,128)(2,1)} %param.16) | copy-start | bytes 1179652
  1012.0 36.8 %copy-start.41 = (f32[128]{0:T(128)S(1)}, f32[128]{0:T(128)}, u32[]{:S(2)}) copy-start(f32[128]{0:T(128)} %copy-done.40) | copy-start | bytes 1540
  1013.7 36.5 %copy-start.7 = (f32[128,1536]{1,0:T(8,128)S(1)}, f32[128,1536]{1,0:T(8,128)}, u32[]{:S(2)}) copy-start(f32[128,1536]{1,0:T(8,128)} %get-tuple-element.49) | copy-start | bytes 2359300
  1013.7 36.5 %copy-start.43 = (f32[128]{0:T(128)S(1)}, f32[128]{0:T(128)}, u32[]{:S(2)}) copy-start(f32[128]{0:T(128)} %get-tuple-element.78) | copy-start | bytes 1540
  1013.7 38.9 %copy-start.37 = (f32[1536]{0:T(1024)S(1)}, f32[1536]{0:T(1024)}, u32[]{:S(2)}) copy-start(f32[1536]{0:T(1024)} %get-tuple-element.36) | copy-start | bytes 18436
  (11 other events, 10.6 us)
Sparse Core Ops, SparseCore 0:
  11.8 20.8 all-gather.5
  47.0 37.9 reduce-scatter.5
  88.8 97.3 all-gather.7
  189.3 94.1 all-gather.9
  298.6 113.6 reduce-scatter.11
  496.4 159.3 reduce-scatter.9
  662.9 154.8 reduce-scatter.7
  820.8 19.1 all-gather.11
  842.8 31.3 all-reduce.7
  879.0 128.9 all-reduce.11
  1010.5 38.2 reduce-scatter.13
  1052.4 68.7 all-reduce.9
